TPU v7x, 32 devices: a whole 2x2x4 slice. The times are simulated.
32 devices in a mesh: dp: 4 (over x, core), mp: 8 (over z, y).
Axes of the slice: x: 2, y: 2, z: 4, core: 2. Of those that a mesh axis runs over, the one named last changes fastest.
Arguments:
- block_input: bfloat16 [4096, 2048], P(('dp', 'mp')), may hold values from -6 to 6
- out_cotangent: bfloat16 [4096, 2048], P(('dp', 'mp')), may hold values from -6 to 6
- segments: int32 [4, 1024], P('dp'), may hold values from 0 to 3, never falling along the last dimension, each value on 1 to 512 neighbouring positions
- domain_tags: int32 [4], P('dp'), may hold values from 0 to 7
- counts: int32 [8], replicated, may hold values from 1 to 4
- attn_gain: float32 [2048], replicated, may hold values from 0.5 to 1.5
- mlp_gain: float32 [2048], replicated, may hold values from 0.5 to 1.5
- norm_gain: float32 [2048], P('mp'), may hold values from 0.5 to 1.5
- bound_table: float32 [24, 2048], P(None, 'mp'), may hold values from -4 to 4
- w_input: bfloat16 [2048, 2048], P(None, 'mp'), may hold values from -0.125 to 0.125
- w_forget: bfloat16 [2048, 2048], P(None, 'mp'), may hold values from -0.125 to 0.125
- w_gate_mix: bfloat16 [2048, 2048], P(None, 'mp'), may hold values from -0.125 to 0.125
- w_out: bfloat16 [2048, 2048], P('mp'), may hold values from -0.1875 to 0.1875
- w_glu_gate: bfloat16 [2048, 5632], P(None, 'mp'), may hold values from -0.125 to 0.125
- w_glu_up: bfloat16 [2048, 5632], P(None, 'mp'), may hold values from -0.125 to 0.125
- w_glu_down: bfloat16 [5632, 2048], P('mp'), may hold values from -0.109375 to 0.109375
Outputs:
- result: bfloat16 [4096, 2048], P(('dp', 'mp'))
- grad_block_input: float32 [4096, 2048], P(('dp', 'mp'))
- grad_attn_gain: float32 [2048], replicated
- grad_mlp_gain: float32 [2048], replicated
- grad_norm_gain: float32 [2048], replicated
- grad_bound_table: float32 [24, 2048], replicated
- grad_input: float32 [2048, 2048], P('dp', 'mp')
- grad_forget: float32 [2048, 2048], P('dp', 'mp')
- grad_gate_mix: float32 [2048, 2048], P('dp', 'mp')
- grad_out: float32 [2048, 2048], P('mp', 'dp')
- grad_glu_gate: float32 [2048, 5632], P('dp', 'mp')
- grad_glu_up: float32 [2048, 5632], P('dp', 'mp')
- grad_glu_down: float32 [5632, 2048], P('mp', 'dp')
Inputs may be any that keep to these rules, and one draw needn't show every extreme that they name: `segments`: along each row the document ids never fall; each document has at least one position.
All inputs are finite; a program needn't handle non-finite values.
Results may differ from a plain program's by a relative error of at most 0.022.
Values may be sent and summed in bfloat16 or wider, within the bound.
No kernel may reach another device: no remote copies, remote signals or barrier semaphores. Data moves between devices by JAX's collectives and lax.ppermute only.
A program may use at most 320 MiB of HBM per device.

v0:
```python
import jax
import jax.numpy as jnp
from jax import lax
from jax.sharding import PartitionSpec as P

NLAYER = 24
LAYER = 20
LEN = 1024
BLK = 128
NDOM = 8
EPS = 1e-06
HIGH = lax.Precision.HIGHEST


def inverse_rms(rows):
    return lax.rsqrt(jnp.mean(rows * rows, axis=1, keepdims=True) + EPS)


def silu_slope(value):
    sig = jax.nn.sigmoid(value)
    return sig * (1.0 + value * (1.0 - sig))


def norm_back(grad_normed, rows, inverse, gain):
    scaled = grad_normed * gain
    unit = rows * inverse
    back = inverse * (scaled - unit * jnp.mean(scaled * unit, axis=1, keepdims=True))
    return (back, jnp.sum(grad_normed * unit, axis=0))


def block_terms(log_blk, reset_blk, lower):
    cum_log = jnp.einsum("csu,tu->cst", log_blk, lower, precision=HIGH)
    cum_reset = jnp.einsum("su,tu->st", reset_blk, lower, precision=HIGH)
    same = (cum_reset[:, :, None] == cum_reset[:, None, :]) & (lower[None] > 0.5)
    spread = jnp.minimum(cum_log[:, :, :, None] - cum_log[:, :, None, :], 0.0)
    weight = jnp.where(same[None], jnp.exp(spread), 0.0)
    return (weight, cum_log, cum_reset)


def local(
    block_input,
    out_cotangent,
    segments,
    domain_tags,
    counts,
    attn_gain,
    mlp_gain,
    norm_gain,
    bound_table,
    w_input,
    w_forget,
    w_gate_mix,
    w_out,
    w_glu_gate,
    w_glu_up,
    w_glu_down,
):
    rows_dev, width = block_input.shape
    chans = w_input.shape[1]
    units = w_glu_gate.shape[1]
    seqs = segments.shape[0]
    total_rows = seqs * LEN
    nblk = LEN // BLK
    mp_index = lax.axis_index("mp")
    own_start = mp_index * rows_dev
    own_rows = block_input.astype(jnp.float32)
    own_inv1 = inverse_rms(own_rows)
    input_all = lax.all_gather(block_input, "mp", axis=0, tiled=True)
    input_all_f = input_all.astype(jnp.float32)
    normed_all = (input_all_f * inverse_rms(input_all_f) * attn_gain).astype(jnp.bfloat16)
    w_mix = jnp.concatenate([w_input, w_forget, w_gate_mix], axis=1)
    pre_mix = jnp.einsum("td,dc->ct", normed_all, w_mix, preferred_element_type=jnp.float32)
    pre_i = pre_mix[:chans].reshape(chans, seqs, LEN)
    pre_f = pre_mix[chans : 2 * chans].reshape(chans, seqs, LEN)
    pre_g = pre_mix[2 * chans :]
    shares = jax.nn.softmax(bound_table, axis=0)
    layer_ids = jnp.arange(NLAYER)
    pick = ((layer_ids >= 1) & (layer_ids <= LAYER)).astype(jnp.float32)[:, None]
    bound_vec = jnp.sum(shares * pick, axis=0)
    bound = bound_vec[:, None, None]
    sig_f = jax.nn.sigmoid(pre_f)
    forget = bound + (1.0 - bound) * sig_f
    act_i = jax.nn.silu(pre_i)
    update = act_i * (1.0 - forget)
    keep = jnp.concatenate(
        [
            jnp.zeros((seqs, 1), jnp.float32),
            (segments[:, 1:] == segments[:, :-1]).astype(jnp.float32),
        ],
        axis=1,
    )
    positions = jnp.arange(BLK)
    lower = (positions[None, :] <= positions[:, None]).astype(jnp.float32)

    def split_blocks(arr):
        arr = arr.reshape(arr.shape[:-1] + (nblk, BLK))
        return jnp.moveaxis(arr, -2, 0)

    def join_blocks(arr):
        arr = jnp.moveaxis(arr, 0, -2)
        return arr.reshape(arr.shape[:-2] + (LEN,))

    log_blocks = split_blocks(jnp.log(forget))
    reset_blocks = split_blocks(1.0 - keep)

    def forward_step(state, blk):
        log_blk, reset_blk, update_blk = blk
        weight, cum_log, cum_reset = block_terms(log_blk, reset_blk, lower)
        lead = jnp.where(cum_reset[None] == 0.0, jnp.exp(cum_log), 0.0)
        states_blk = (
            jnp.einsum("cstu,csu->cst", weight, update_blk, precision=HIGH)
            + lead * state[:, :, None]
        )
        return (states_blk[:, :, -1], states_blk)

    _, state_blocks = lax.scan(
        forward_step,
        jnp.zeros((chans, seqs), jnp.float32),
        (log_blocks, reset_blocks, split_blocks(update)),
    )
    states3 = join_blocks(state_blocks)
    states = states3.reshape(chans, total_rows)
    square_sum = lax.psum(jnp.sum(states * states, axis=0), "mp")
    rec_inv = lax.rsqrt(square_sum / width + EPS)
    unit_states = states * rec_inv[None, :]
    act_g = jax.nn.silu(pre_g)
    gated = (unit_states * norm_gain[:, None] * act_g).astype(jnp.bfloat16)
    partial_mix = jnp.einsum("ct,cd->td", gated, w_out, preferred_element_type=jnp.float32)
    middle_all = input_all_f + lax.psum(partial_mix.astype(jnp.bfloat16), "mp").astype(jnp.float32)
    normed_two_all = (middle_all * inverse_rms(middle_all) * mlp_gain).astype(jnp.bfloat16)
    middle = lax.dynamic_slice_in_dim(middle_all, own_start, rows_dev, 0)
    own_inv2 = inverse_rms(middle)
    w_glu = jnp.concatenate([w_glu_gate, w_glu_up], axis=1)
    gate_up = jnp.dot(normed_two_all, w_glu, preferred_element_type=jnp.float32)
    gate = gate_up[:, :units]
    up = gate_up[:, units:]
    act_gate = jax.nn.silu(gate)
    hidden = (act_gate * up).astype(jnp.bfloat16)
    piece = hidden
    final = middle + lax.psum_scatter(
        jnp.dot(piece, w_glu_down, preferred_element_type=jnp.float32).astype(jnp.bfloat16),
        "mp",
        scatter_dimension=0,
        tiled=True,
    ).astype(jnp.float32)
    result = final.astype(jnp.bfloat16)
    domain_hit = (domain_tags[:, None] == jnp.arange(NDOM)[None, :]).astype(jnp.float32)
    seq_count = jnp.dot(domain_hit, counts.astype(jnp.float32)[:, None], precision=HIGH)[:, 0]
    seq_weight = lax.rsqrt(seq_count)
    cot_all = lax.all_gather(out_cotangent, "mp", axis=0, tiled=True)
    grad_all = (
        cot_all.astype(jnp.float32).reshape(seqs, LEN, width) * seq_weight[:, None, None]
    ).reshape(total_rows, width)
    grad_all_b = grad_all.astype(jnp.bfloat16)
    grad_own = lax.dynamic_slice_in_dim(grad_all, own_start, rows_dev, 0)
    grad_hidden = jnp.einsum(
        "td,fd->tf", grad_all_b, w_glu_down, preferred_element_type=jnp.float32
    )
    down_term = jnp.einsum("tf,td->fd", hidden, grad_all_b, preferred_element_type=jnp.float32)
    grad_gate = grad_hidden * up * silu_slope(gate)
    grad_up = grad_hidden * act_gate
    grad_gate_up = jnp.concatenate([grad_gate, grad_up], axis=1).astype(jnp.bfloat16)
    piece = grad_gate_up
    grad_normed_two = lax.psum_scatter(
        jnp.einsum("tf,df->td", piece, w_glu, preferred_element_type=jnp.float32).astype(
            jnp.bfloat16
        ),
        "mp",
        scatter_dimension=0,
        tiled=True,
    ).astype(jnp.float32)
    back_two, mlp_gain_term = norm_back(grad_normed_two, middle, own_inv2, mlp_gain)
    grad_middle = grad_own + back_two
    middle_grad_all = lax.all_gather(grad_middle.astype(jnp.bfloat16), "mp", axis=0, tiled=True)
    grad_gated = jnp.einsum("td,cd->ct", middle_grad_all, w_out, preferred_element_type=jnp.float32)
    out_term = jnp.einsum("ct,td->cd", gated, middle_grad_all, preferred_element_type=jnp.float32)
    grad_unit = grad_gated * norm_gain[:, None] * act_g
    norm_gain_term = jnp.sum(grad_gated * unit_states * act_g, axis=1)
    grad_pre_g = grad_gated * unit_states * norm_gain[:, None] * silu_slope(pre_g)
    inner = lax.psum(jnp.sum(grad_unit * unit_states, axis=0), "mp")
    grad_states = rec_inv[None, :] * (grad_unit - unit_states * (inner / width)[None, :])
    forget_heads = split_blocks(forget)[..., 0]
    keep_heads = split_blocks(keep)[..., 0]

    def backward_step(carry, blk):
        log_blk, reset_blk, grad_blk, forget_head, keep_head = blk
        weight, cum_log, cum_reset = block_terms(log_blk, reset_blk, lower)
        trailing = jnp.where(
            (cum_reset == cum_reset[:, -1:])[None], jnp.exp(cum_log[:, :, -1:] - cum_log), 0.0
        )
        total = (
            jnp.einsum("cstu,cst->csu", weight, grad_blk, precision=HIGH)
            + trailing * carry[:, :, None]
        )
        return (forget_head * keep_head[None] * total[:, :, 0], total)

    _, grad_blocks = lax.scan(
        backward_step,
        jnp.zeros((chans, seqs), jnp.float32),
        (
            log_blocks,
            reset_blocks,
            split_blocks(grad_states.reshape(chans, seqs, LEN)),
            forget_heads,
            keep_heads,
        ),
        reverse=True,
    )
    grad_update = join_blocks(grad_blocks)
    prior = jnp.concatenate([jnp.zeros((chans, seqs, 1), jnp.float32), states3[:, :, :-1]], axis=2)
    grad_forget = grad_update * keep[None] * prior - grad_update * act_i
    grad_pre_i = grad_update * (1.0 - forget) * silu_slope(pre_i)
    grad_pre_f = grad_forget * (1.0 - bound) * sig_f * (1.0 - sig_f)
    bound_grad = jnp.sum(grad_forget * (1.0 - sig_f), axis=(1, 2))
    pick_grad = pick * bound_grad[None, :]
    table_term = shares * (pick_grad - jnp.sum(shares * pick_grad, axis=0, keepdims=True))
    grad_pre = jnp.concatenate(
        [grad_pre_i.reshape(chans, total_rows), grad_pre_f.reshape(chans, total_rows), grad_pre_g],
        axis=0,
    ).astype(jnp.bfloat16)
    piece = grad_pre
    grad_normed = lax.psum_scatter(
        jnp.einsum("ct,dc->td", piece, w_mix, preferred_element_type=jnp.float32).astype(
            jnp.bfloat16
        ),
        "mp",
        scatter_dimension=0,
        tiled=True,
    ).astype(jnp.float32)
    back_one, attn_gain_term = norm_back(grad_normed, own_rows, own_inv1, attn_gain)
    grad_block_input = grad_middle + back_one
    mix_part = jnp.einsum("tk,ct->kc", normed_all, grad_pre, preferred_element_type=jnp.float32)
    glu_part = jnp.einsum(
        "tk,tf->kf", normed_two_all, grad_gate_up, preferred_element_type=jnp.float32
    )
    weight_grads = lax.psum_scatter(
        jnp.concatenate([mix_part, glu_part], axis=1).astype(jnp.bfloat16),
        "dp",
        scatter_dimension=0,
        tiled=True,
    ).astype(jnp.float32)
    out_grad, down_grad = (
        lax.psum_scatter(
            out_term.astype(jnp.bfloat16), "dp", scatter_dimension=1, tiled=True
        ).astype(jnp.float32),
        lax.psum_scatter(
            down_term.astype(jnp.bfloat16), "dp", scatter_dimension=1, tiled=True
        ).astype(jnp.float32),
    )
    groups = lax.axis_size("mp")
    onehot = (jnp.arange(groups) == mp_index).astype(jnp.float32)
    norm_full = (onehot[:, None] * norm_gain_term[None, :]).reshape(width)
    table_full = (table_term[:, None, :] * onehot[None, :, None]).reshape(NLAYER, width)
    attn_sum, mlp_sum, norm_sum, table_sum = lax.psum(
        (attn_gain_term, mlp_gain_term, norm_full, table_full), ("dp", "mp")
    )
    grad_input = weight_grads[:, :chans]
    grad_forget_w = weight_grads[:, chans : 2 * chans]
    grad_gate_mix = weight_grads[:, 2 * chans : 3 * chans]
    grad_glu_gate = weight_grads[:, 3 * chans : 3 * chans + units]
    grad_glu_up = weight_grads[:, 3 * chans + units :]
    return (
        result,
        grad_block_input,
        attn_sum,
        mlp_sum,
        norm_sum,
        table_sum,
        grad_input,
        grad_forget_w,
        grad_gate_mix,
        out_grad,
        grad_glu_gate,
        grad_glu_up,
        down_grad,
    )


def solution(mesh):
    placed = (
        P(("dp", "mp"), None),
        P(("dp", "mp"), None),
        P("dp", None),
        P("dp"),
        P(),
        P(),
        P(),
        P("mp"),
        P(None, "mp"),
        P(None, "mp"),
        P(None, "mp"),
        P(None, "mp"),
        P("mp", None),
        P(None, "mp"),
        P(None, "mp"),
        P("mp", None),
    )
    return jax.shard_map(
        local,
        mesh=mesh,
        in_specs=placed,
        out_specs=(
            P(("dp", "mp"), None),
            P(("dp", "mp"), None),
            P(),
            P(),
            P(),
            P(),
            P("dp", "mp"),
            P("dp", "mp"),
            P("dp", "mp"),
            P("mp", "dp"),
            P("dp", "mp"),
            P("dp", "mp"),
            P("mp", "dp"),
        ),
        check_vma=False,
    )
```

profile of v0, /device:TPU:10, one launch (start us, length us, event | category | flops | bytes accessed | tf_op | source)
XLA Modules:
  0.0 1434.1 jit_solution(5197083218827090929)
XLA Ops:
  17.3 66.8 %all-gather.4.cloned.1.call-done = bf16[1024,2048]{1,0:T(8,128)(2,1)} async-done(((bf16[128,2048]{1,0:T(8,128)(2,1)}), bf16[1024,2048]{1,0:T(8,128)(2,1)}) %all-gather.4.cloned.1.call-update) | async-done | bytes 4194320 | tf_op jit(solution)/shard_map/all_gather | solution.py:68
  100.1 259.9 %while.32 = (s32[]{:T(128)}, f32[256,1]{0,1:T(1,128)S(1)}, f32[8,256,1,128]{1,3,2,0:T(8,128)}, f32[8,1,128]{2,1,0:T(1,128)S(1)}, f32[8,256,1,128]{3,2,1,0:T(1,128)}, /*index=5*/f32[8,256,1,128]{3,2,1,0:T(1,128)}, s32[]{:T(128)}) while((s32[]{:T(128)}, f32[256,1]{0,1:T(1,128)S(1)}, f32[8,256,1,128]{1,3,2,0:T(8,128)}, ...), condition=%wide.region_5.6_spmd.clone.clone, body=%wide.region_4.0_spmd.clone.clone.sunk | while | flops 113787008 | bytes 2398181 | solution.py:116
  102.0 28.5 %fusion.137 = f32[256,1,128]{2,1,0:T(1,128)S(1)} fusion(f32[256,128]{1,0:T(8,128)S(1)} %copy.93, pred[128,128]{1,0:T(8,128)(4,1)S(1)} %fusion.136, f32[8,256,1,128]{3,2,1,0:T(1,128)} %get-tuple-element.526, s32[]{:T(128)S(6)} %copy.104), kind=kOutput, calls=%fused_computation.2.clone.1 | convolution fusion | flops 62914560 | bytes 540676 | tf_op jit(solution)/shard_map/while/body/eval_jaxpr/cstu,csu->cst/dot_general | solution.py:111
  133.1 28.5 %fusion.137 = f32[256,1,128]{2,1,0:T(1,128)S(1)} fusion(f32[256,128]{1,0:T(8,128)S(1)} %copy.93, pred[128,128]{1,0:T(8,128)(4,1)S(1)} %fusion.136, f32[8,256,1,128]{3,2,1,0:T(1,128)} %get-tuple-element.526, s32[]{:T(128)S(6)} %copy.104), kind=kOutput, calls=%fused_computation.2.clone.1 | convolution fusion | flops 62914560 | bytes 540676 | tf_op jit(solution)/shard_map/while/body/eval_jaxpr/cstu,csu->cst/dot_general | solution.py:111
  164.3 28.5 %fusion.137 = f32[256,1,128]{2,1,0:T(1,128)S(1)} fusion(f32[256,128]{1,0:T(8,128)S(1)} %copy.93, pred[128,128]{1,0:T(8,128)(4,1)S(1)} %fusion.136, f32[8,256,1,128]{3,2,1,0:T(1,128)} %get-tuple-element.526, s32[]{:T(128)S(6)} %copy.104), kind=kOutput, calls=%fused_computation.2.clone.1 | convolution fusion | flops 62914560 | bytes 540676 | tf_op jit(solution)/shard_map/while/body/eval_jaxpr/cstu,csu->cst/dot_general | solution.py:111
  195.4 28.5 %fusion.137 = f32[256,1,128]{2,1,0:T(1,128)S(1)} fusion(f32[256,128]{1,0:T(8,128)S(1)} %copy.93, pred[128,128]{1,0:T(8,128)(4,1)S(1)} %fusion.136, f32[8,256,1,128]{3,2,1,0:T(1,128)} %get-tuple-element.526, s32[]{:T(128)S(6)} %copy.104), kind=kOutput, calls=%fused_computation.2.clone.1 | convolution fusion | flops 62914560 | bytes 540676 | tf_op jit(solution)/shard_map/while/body/eval_jaxpr/cstu,csu->cst/dot_general | solution.py:111
  226.6 28.5 %fusion.137 = f32[256,1,128]{2,1,0:T(1,128)S(1)} fusion(f32[256,128]{1,0:T(8,128)S(1)} %copy.93, pred[128,128]{1,0:T(8,128)(4,1)S(1)} %fusion.136, f32[8,256,1,128]{3,2,1,0:T(1,128)} %get-tuple-element.526, s32[]{:T(128)S(6)} %copy.104), kind=kOutput, calls=%fused_computation.2.clone.1 | convolution fusion | flops 62914560 | bytes 540676 | tf_op jit(solution)/shard_map/while/body/eval_jaxpr/cstu,csu->cst/dot_general | solution.py:111
  257.7 28.5 %fusion.137 = f32[256,1,128]{2,1,0:T(1,128)S(1)} fusion(f32[256,128]{1,0:T(8,128)S(1)} %copy.93, pred[128,128]{1,0:T(8,128)(4,1)S(1)} %fusion.136, f32[8,256,1,128]{3,2,1,0:T(1,128)} %get-tuple-element.526, s32[]{:T(128)S(6)} %copy.104), kind=kOutput, calls=%fused_computation.2.clone.1 | convolution fusion | flops 62914560 | bytes 540676 | tf_op jit(solution)/shard_map/while/body/eval_jaxpr/cstu,csu->cst/dot_general | solution.py:111
  288.9 28.5 %fusion.137 = f32[256,1,128]{2,1,0:T(1,128)S(1)} fusion(f32[256,128]{1,0:T(8,128)S(1)} %copy.93, pred[128,128]{1,0:T(8,128)(4,1)S(1)} %fusion.136, f32[8,256,1,128]{3,2,1,0:T(1,128)} %get-tuple-element.526, s32[]{:T(128)S(6)} %copy.104), kind=kOutput, calls=%fused_computation.2.clone.1 | convolution fusion | flops 62914560 | bytes 540676 | tf_op jit(solution)/shard_map/while/body/eval_jaxpr/cstu,csu->cst/dot_general | solution.py:111
  320.0 28.5 %fusion.137 = f32[256,1,128]{2,1,0:T(1,128)S(1)} fusion(f32[256,128]{1,0:T(8,128)S(1)} %copy.93, pred[128,128]{1,0:T(8,128)(4,1)S(1)} %fusion.136, f32[8,256,1,128]{3,2,1,0:T(1,128)} %get-tuple-element.526, s32[]{:T(128)S(6)} %copy.104), kind=kOutput, calls=%fused_computation.2.clone.1 | convolution fusion | flops 62914560 | bytes 540676 | tf_op jit(solution)/shard_map/while/body/eval_jaxpr/cstu,csu->cst/dot_general | solution.py:111
  395.8 145.9 %all-reduce.5.cloned.1.call-done = bf16[1024,2048]{1,0:T(8,128)(2,1)} async-done(((bf16[1024,2048]{1,0:T(8,128)(2,1)}), bf16[1024,2048]{1,0:T(8,128)(2,1)}) %all-reduce.5.cloned.1.call-update) | async-done | bytes 4194320 | tf_op jit(solution)/shard_map/psum | solution.py:129
  561.3 56.1 %all-gather.6.cloned.1.call-done = bf16[1024,2048]{1,0:T(8,128)(2,1)} async-done(((bf16[128,2048]{1,0:T(8,128)(2,1)}), bf16[1024,2048]{1,0:T(8,128)(2,1)}) %all-gather.6.cloned.1.call-update) | async-done | bytes 4194320 | tf_op jit(solution)/shard_map/all_gather | solution.py:150
  647.5 79.2 %reduce-scatter.9.cloned.1.call-done = bf16[128,2048]{1,0:T(8,128)(2,1)} async-done(((bf16[1024,2048]{1,0:T(8,128)(2,1)}), bf16[128,2048]{1,0:T(8,128)(2,1)}) %reduce-scatter.9.cloned.1.call-update) | async-done | bytes 524304 | tf_op jit(solution)/shard_map/reduce_scatter | solution.py:164
  747.4 56.4 %all-gather.8.cloned.1.call-done = bf16[1024,2048]{1,0:T(8,128)(2,1)} async-done(((bf16[128,2048]{1,0:T(8,128)(2,1)}), bf16[1024,2048]{1,0:T(8,128)(2,1)}) %all-gather.8.cloned.1.call-update) | async-done | bytes 4194320 | tf_op jit(solution)/shard_map/all_gather | solution.py:174
  835.1 182.9 %while.33 = (s32[]{:T(128)}, f32[256,1]{0,1:T(1,128)S(1)}, f32[8,256,1,128]{1,3,2,0:T(8,128)}, f32[8,256,1]{1,2,0:T(1,128)S(1)}, f32[8,1]{0,1:T(1,128)S(1)}, /*i...) while((s32[]{:T(128)}, f32[256,1]{0,1:T(1,128)S(1)}, ...), condition=%wide.region_18.19_spmd.clone.clone, body=%wide.region_17.18_spmd.clone.clone.sunk | while | flops 113853312 | bytes 2405947 | solution.py:197
  838.1 17.7 %fusion.148 = f32[256,1,128]{2,1,0:T(1,128)S(1)} fusion(f32[256,128]{1,0:T(8,128)S(1)} %copy.95, pred[128,128]{1,0:T(8,128)(4,1)S(1)} %fusion.147, f32[8,256,1,128]{3,2,1,0:T(1,128)} %get-tuple-element.557, s32[]{:T(128)S(6)} %sub.280), kind=kOutput, calls=%fused_computation.30.clone.1 | convolution fusion | flops 62914560 | bytes 540676 | tf_op jit(solution)/shard_map/while/body/eval_jaxpr/cstu,cst->csu/dot_general | solution.py:192
  861.0 17.7 %fusion.148 = f32[256,1,128]{2,1,0:T(1,128)S(1)} fusion(f32[256,128]{1,0:T(8,128)S(1)} %copy.95, pred[128,128]{1,0:T(8,128)(4,1)S(1)} %fusion.147, f32[8,256,1,128]{3,2,1,0:T(1,128)} %get-tuple-element.557, s32[]{:T(128)S(6)} %sub.280), kind=kOutput, calls=%fused_computation.30.clone.1 | convolution fusion | flops 62914560 | bytes 540676 | tf_op jit(solution)/shard_map/while/body/eval_jaxpr/cstu,cst->csu/dot_general | solution.py:192
  929.4 17.7 %fusion.148 = f32[256,1,128]{2,1,0:T(1,128)S(1)} fusion(f32[256,128]{1,0:T(8,128)S(1)} %copy.95, pred[128,128]{1,0:T(8,128)(4,1)S(1)} %fusion.147, f32[8,256,1,128]{3,2,1,0:T(1,128)} %get-tuple-element.557, s32[]{:T(128)S(6)} %sub.280), kind=kOutput, calls=%fused_computation.30.clone.1 | convolution fusion | flops 62914560 | bytes 540676 | tf_op jit(solution)/shard_map/while/body/eval_jaxpr/cstu,cst->csu/dot_general | solution.py:192
  997.9 17.7 %fusion.148 = f32[256,1,128]{2,1,0:T(1,128)S(1)} fusion(f32[256,128]{1,0:T(8,128)S(1)} %copy.95, pred[128,128]{1,0:T(8,128)(4,1)S(1)} %fusion.147, f32[8,256,1,128]{3,2,1,0:T(1,128)} %get-tuple-element.557, s32[]{:T(128)S(6)} %sub.280), kind=kOutput, calls=%fused_computation.30.clone.1 | convolution fusion | flops 62914560 | bytes 540676 | tf_op jit(solution)/shard_map/while/body/eval_jaxpr/cstu,cst->csu/dot_general | solution.py:192
  1077.6 46.3 %reduce-scatter.11.cloned.1.call-done = bf16[128,2048]{1,0:T(8,128)(2,1)} async-done(((bf16[1024,2048]{1,0:T(8,128)(2,1)}), bf16[128,2048]{1,0:T(8,128)(2,1)}) %reduce-scatter.11.cloned.1.call-update) | async-done | bytes 524304 | tf_op jit(solution)/shard_map/reduce_scatter | solution.py:222
  1125.4 42.5 %all-reduce.1 = (f32[2048]{0:T(1024)}, f32[2048]{0:T(1024)}, f32[2048]{0:T(1024)}) all-reduce(f32[2048]{0:T(1024)S(1)} %get-tuple-element.358, f32[2048]{0:T(1024)S(1)} %get-tuple-element.354, f32[2048]{0:T(1024)S(1)} %mul.516), channel_id=1, replica_groups=mesh['dp'=4,'mp'=8] {'dp','mp'}, use_global_device_ids=true, to_apply=%region_22.23 | all-reduce | flops 6144 | bytes 49152 | tf_op jit(solution)/shard_map/psum | solution.py:254
  1167.8 48.6 %reduce-scatter.7.cloned.1.call-done = bf16[128,2048]{1,0:T(8,128)(2,1)} async-done(((bf16[1024,2048]{1,0:T(8,128)(2,1)}), bf16[128,2048]{1,0:T(8,128)(2,1)}) %reduce-scatter.7.cloned.1.call-update) | async-done | bytes 524304 | tf_op jit(solution)/shard_map/reduce_scatter | solution.py:140
  1220.1 72.7 %reduce-scatter.13.cloned.1.call-done = bf16[512,2176]{0,1:T(8,128)(2,1)} async-done(((bf16[2048,2176]{0,1:T(8,128)(2,1)}), bf16[512,2176]{0,1:T(8,128)(2,1)}) %reduce-scatter.13.cloned.1.call-update) | async-done | bytes 2228240 | tf_op jit(solution)/shard_map/reduce_scatter | solution.py:236
  1302.5 123.1 %all-reduce.7.cloned.1.call-done = f32[24,2048]{1,0:T(8,128)} async-done(((f32[24,2048]{1,0:T(8,128)}), f32[24,2048]{1,0:T(8,128)}) %all-reduce.7.cloned.1.call-update) | async-done | bytes 196624 | tf_op jit(solution)/shard_map/psum | solution.py:254
  (374 shorter events, 369.1 us)
Async XLA Ops:
  7.2 610.2 %copy-start = (bf16[704,2048]{1,0:T(8,128)(2,1)S(1)}, bf16[704,2048]{1,0:T(8,128)(2,1)}, u32[]{:S(2)}) copy-start(bf16[704,2048]{1,0:T(8,128)(2,1)} %param.35) | copy-start | bytes 8650756
  7.2 76.9 %all-gather.4.cloned.1.call-start = ((), (), s32[]{:S(2)}) async-start(), calls=%async_computation.6 | async-start | bytes 4718592 | tf_op jit(solution)/shard_map/all_gather | solution.py:68
  7.9 533.8 %all-reduce.5.cloned.1.call-start = ((), (), s32[]{:S(2)}) async-start(), calls=%async_computation.7 | async-start | bytes 8388608 | tf_op jit(solution)/shard_map/psum | solution.py:129
  11.4 81.7 %copy-start.24 = (f32[256]{0:T(256)}, f32[256]{0:T(256)S(1)}, u32[]{:S(2)}) copy-start(f32[256]{0:T(256)S(1)} %multiply_reduce_fusion.4) | copy-start | bytes 3076
  11.4 81.7 %copy-start.22 = (f32[256]{0:T(256)}, f32[256]{0:T(256)S(1)}, u32[]{:S(2)}) copy-start(f32[256]{0:T(256)S(1)} %broadcast_subtract_fusion.1) | copy-start | bytes 3076
  13.8 73.5 %copy-start.18 = (f32[2048]{0:T(1024)S(1)}, f32[2048]{0:T(1024)}, u32[]{:S(2)}) copy-start(f32[2048]{0:T(1024)} %param.25) | copy-start | bytes 24580
  100.1 280.5 %copy-start.32 = (f32[256]{0:T(256)S(1)}, f32[256]{0:T(256)}, u32[]{:S(2)}) copy-start(f32[256]{0:T(256)} %param.27) | copy-start | bytes 3076
  387.1 230.3 %all-gather.6.cloned.1.call-start = ((), (), s32[]{:S(2)}) async-start(), calls=%async_computation.9 | async-start | bytes 4718592 | tf_op jit(solution)/shard_map/all_gather | solution.py:150
  387.8 338.9 %reduce-scatter.9.cloned.1.call-start = ((), (), s32[]{:S(2)}) async-start(), calls=%async_computation.10 | async-start | bytes 4718592 | tf_op jit(solution)/shard_map/reduce_scatter | solution.py:164
  395.8 154.1 %copy-start.17 = (f32[2048]{0:T(1024)S(1)}, f32[2048]{0:T(1024)}, u32[]{:S(2)}) copy-start(f32[2048]{0:T(1024)} %param.26) | copy-start | bytes 24580
  541.7 8.2 copy-start.4
  541.7 8.2 copy-start.9
  639.4 164.4 %all-gather.8.cloned.1.call-start = ((), (), s32[]{:S(2)}) async-start(), calls=%async_computation.11 | async-start | bytes 4718592 | tf_op jit(solution)/shard_map/all_gather | solution.py:174
  731.4 340.9 %reduce-scatter.17.cloned.1.call-start = ((), (), s32[]{:S(2)}) async-start(), calls=%async_computation.16 | async-start | bytes 3604480 | tf_op jit(solution)/shard_map/reduce_scatter | solution.py:246
  739.3 336.5 %reduce-scatter.15.cloned.1.call-start = ((), (), s32[]{:S(2)}) async-start(), calls=%async_computation.15 | async-start | bytes 1310720 | tf_op jit(solution)/shard_map/reduce_scatter | solution.py:243
  834.0 289.9 %reduce-scatter.11.cloned.1.call-start = ((), (), s32[]{:S(2)}) async-start(), calls=%async_computation.12 | async-start | bytes 4718592 | tf_op jit(solution)/shard_map/reduce_scatter | solution.py:222
  1035.5 180.9 %reduce-scatter.7.cloned.1.call-start = ((), (), s32[]{:S(2)}) async-start(), calls=%async_computation.8 | async-start | bytes 4718592 | tf_op jit(solution)/shard_map/reduce_scatter | solution.py:140
  1042.0 13.6 copy-start.19
  1042.1 13.6 copy-start.31
  1042.1 250.7 %reduce-scatter.13.cloned.1.call-start = ((), (), s32[]{:S(2)}) async-start(), calls=%async_computation.14 | async-start | bytes 11141120 | tf_op jit(solution)/shard_map/reduce_scatter | solution.py:236
  1042.1 13.6 copy-start.5
  1042.1 13.6 copy-start.14
  1042.1 13.6 copy-start.16
  1071.1 354.5 %all-reduce.7.cloned.1.call-start = ((), (), s32[]{:S(2)}) async-start(), calls=%async_computation.13 | async-start | bytes 393216 | tf_op jit(solution)/shard_map/psum | solution.py:254
  (24 other events, 77.7 us)
Sparse Core Ops, SparseCore 0:
  10.2 73.8 all-gather.3
  387.2 154.4 all-reduce.4
  543.8 73.4 all-gather.5
  639.5 87.1 reduce-scatter.8
  731.5 72.2 all-gather.7
  806.3 34.3 reduce-scatter.16
  843.2 24.8 reduce-scatter.14
  1035.7 88.1 reduce-scatter.10
  1127.5 88.8 reduce-scatter.6
  1219.0 73.6 reduce-scatter.12
  1299.8 125.7 all-reduce.6
where the time goes:
time: 1440 us; the launch traced here: 1430 us
  waiting for transfers between devices  697 us (48%)
  matrix products  468 us (32%)
  other arithmetic  86.1 us (6%)
  local copies, waits for them, and re-layouts  78.9 us (5%)
  blocking collectives  75.7 us (5%)
  between operations  16.1 us (1%)
    dot_general x8, matrix products, forward_step(): jnp.einsum('cstu,csu->cst', weight, update_blk, precision=HIGH)  228 us
    psum x1, waiting for transfers between devices, local(): lax.psum(partial_mix.astype(jnp.bfloat16), 'mp').astype(jnp.float32)  146 us
    dot_general x8, matrix products, backward_step(): jnp.einsum('cstu,cst->csu', weight, grad_blk, precision=HIGH)  142 us
    psum x1, waiting for transfers between devices, local(): lax.psum((attn_gain_term, mlp_gain_term, norm_full, table_full), ('dp', '...  123 us
    reduce_scatter x1, waiting for transfers between devices, local(): lax.psum_scatter(jnp.einsum('tf,df->td', piece, w_glu, preferred_element_...  79.2 us
    reduce_scatter x1, waiting for transfers between devices, local(): lax.psum_scatter(jnp.concatenate([mix_part, glu_part], axis=1).astype(jnp...  72.7 us
    all_gather x1, waiting for transfers between devices, local(): input_all = lax.all_gather(block_input, 'mp', axis=0, tiled=True)  66.8 us
    all_gather x1, waiting for transfers between devices, local(): lax.all_gather(grad_middle.astype(jnp.bfloat16), 'mp', axis=0, tiled=True)  56.4 us
  transfers between devices with their start and end apart: 11, of which 9 were waited for; matrix products, arithmetic and copies ran while one was open for 23% of the time, Pallas kernels for 0%

commit v1 on v0

--- a/solution.py
+++ b/solution.py
@@ -1,3 +1,4 @@
+import functools
 import jax
 import jax.numpy as jnp
 from jax import lax
@@ -10,6 +11,13 @@
 NDOM = 8
 EPS = 1e-06
 HIGH = lax.Precision.HIGHEST
+
+
+def _obtain_layers_all(x_in, across):
+    return jnp.sum(lax.all_gather(x_in, axis_name=across), axis=0)
+
+
+supply_all_spans_for = functools.partial(_obtain_layers_all, across="mp")
 
 
 def inverse_rms(rows):
@@ -126,7 +134,9 @@
     act_g = jax.nn.silu(pre_g)
     gated = (unit_states * norm_gain[:, None] * act_g).astype(jnp.bfloat16)
     partial_mix = jnp.einsum("ct,cd->td", gated, w_out, preferred_element_type=jnp.float32)
-    middle_all = input_all_f + lax.psum(partial_mix.astype(jnp.bfloat16), "mp").astype(jnp.float32)
+    middle_all = input_all_f + supply_all_spans_for(partial_mix.astype(jnp.bfloat16)).astype(
+        jnp.float32
+    )
     normed_two_all = (middle_all * inverse_rms(middle_all) * mlp_gain).astype(jnp.bfloat16)
     middle = lax.dynamic_slice_in_dim(middle_all, own_start, rows_dev, 0)
     own_inv2 = inverse_rms(middle)

time: 1440 us -> 1920 us (1.33)
  waiting for transfers between devices: 697 us -> 1160 us
    all_gather x0 -> x1, waiting for transfers between devices: none -> 629 us  [_obtain_layers_all(): return jnp.sum(lax.all_gather(x_in, axis_name=across), axis=0)]
    psum x1 -> x0, waiting for transfers between devices: 146 us -> none  [local(): lax.psum(partial_mix.astype(jnp.bfloat16), 'mp').astype(jnp.float32)]
  transfers between devices with their start and end apart: 11 -> 11, of which waited for: 9 -> 9; matrix products, arithmetic and copies ran while one was open for 23% -> 18% of each run, Pallas kernels for 0% -> 0%
where the time goes in v1:
time: 1920 us
  waiting for transfers between devices  1160 us (60%)
  matrix products  468 us (24%)
  other arithmetic  101 us (5%)
  local copies, waits for them, and re-layouts  77.8 us (4%)
  blocking collectives  75.6 us (4%)
    all_gather x1, waiting for transfers between devices, _obtain_layers_all(): return jnp.sum(lax.all_gather(x_in, axis_name=across), axis=0)  629 us
    dot_general x8, matrix products, forward_step(): jnp.einsum('cstu,csu->cst', weight, update_blk, precision=HIGH)  228 us
    dot_general x8, matrix products, backward_step(): jnp.einsum('cstu,cst->csu', weight, grad_blk, precision=HIGH)  142 us
    psum x1, waiting for transfers between devices, local(): lax.psum((attn_gain_term, mlp_gain_term, norm_full, table_full), ('dp', '...  123 us
    reduce_scatter x1, waiting for transfers between devices, local(): lax.psum_scatter(jnp.einsum('tf,df->td', piece, w_glu, preferred_element_...  78.8 us
    reduce_scatter x1, waiting for transfers between devices, local(): lax.psum_scatter(jnp.concatenate([mix_part, glu_part], axis=1).astype(jnp...  72.7 us
    all_gather x1, waiting for transfers between devices, local(): input_all = lax.all_gather(block_input, 'mp', axis=0, tiled=True)  66.7 us
    all_gather x1, waiting for transfers between devices, local(): lax.all_gather(grad_middle.astype(jnp.bfloat16), 'mp', axis=0, tiled=True)  56.8 us
  transfers between devices with their start and end apart: 11, of which 9 were waited for; matrix products, arithmetic and copies ran while one was open for 18% of the time, Pallas kernels for 0%

profile of v1, /device:TPU:10, one launch (start us, length us, event | category | flops | bytes accessed | tf_op | source)
XLA Modules:
  0.0 1916.5 jit_solution(16305975826141949225)
XLA Ops:
  17.4 66.7 %all-gather.6.cloned.1.call-done = bf16[1024,2048]{1,0:T(8,128)(2,1)} async-done(((bf16[128,2048]{1,0:T(8,128)(2,1)}), bf16[1024,2048]{1,0:T(8,128)(2,1)}) %all-gather.6.cloned.1.call-update) | async-done | bytes 4194320 | tf_op jit(solution)/shard_map/all_gather | solution.py:76
  100.1 259.8 %while.32 = (s32[]{:T(128)}, f32[256,1]{0,1:T(1,128)S(1)}, f32[8,256,1,128]{1,3,2,0:T(8,128)}, f32[8,1,128]{2,1,0:T(1,128)S(1)}, f32[8,256,1,128]{3,2,1,0:T(1,128)}, /*index=5*/f32[8,256,1,128]{3,2,1,0:T(1,128)}, s32[]{:T(128)}) while((s32[]{:T(128)}, f32[256,1]{0,1:T(1,128)S(1)}, f32[8,256,1,128]{1,3,2,0:T(8,128)}, ...), condition=%wide.region_5.6_spmd.clone.clone, body=%wide.region_4.0_spmd.clone.clone.sunk | while | flops 113787008 | bytes 2399189 | solution.py:124
  101.9 28.5 %fusion.137 = f32[256,1,128]{2,1,0:T(1,128)S(1)} fusion(f32[256,128]{1,0:T(8,128)S(1)} %copy.93, pred[128,128]{1,0:T(8,128)(4,1)S(1)} %fusion.136, f32[8,256,1,128]{3,2,1,0:T(1,128)} %get-tuple-element.526, s32[]{:T(128)} %get-tuple-element.514), kind=kOutput, calls=%fused_computation.2.clone.1 | convolution fusion | flops 62914560 | bytes 541184 | tf_op jit(solution)/shard_map/while/body/eval_jaxpr/cstu,csu->cst/dot_general | solution.py:119
  133.1 28.5 %fusion.137 = f32[256,1,128]{2,1,0:T(1,128)S(1)} fusion(f32[256,128]{1,0:T(8,128)S(1)} %copy.93, pred[128,128]{1,0:T(8,128)(4,1)S(1)} %fusion.136, f32[8,256,1,128]{3,2,1,0:T(1,128)} %get-tuple-element.526, s32[]{:T(128)} %get-tuple-element.514), kind=kOutput, calls=%fused_computation.2.clone.1 | convolution fusion | flops 62914560 | bytes 541184 | tf_op jit(solution)/shard_map/while/body/eval_jaxpr/cstu,csu->cst/dot_general | solution.py:119
  164.2 28.5 %fusion.137 = f32[256,1,128]{2,1,0:T(1,128)S(1)} fusion(f32[256,128]{1,0:T(8,128)S(1)} %copy.93, pred[128,128]{1,0:T(8,128)(4,1)S(1)} %fusion.136, f32[8,256,1,128]{3,2,1,0:T(1,128)} %get-tuple-element.526, s32[]{:T(128)} %get-tuple-element.514), kind=kOutput, calls=%fused_computation.2.clone.1 | convolution fusion | flops 62914560 | bytes 541184 | tf_op jit(solution)/shard_map/while/body/eval_jaxpr/cstu,csu->cst/dot_general | solution.py:119
  195.4 28.5 %fusion.137 = f32[256,1,128]{2,1,0:T(1,128)S(1)} fusion(f32[256,128]{1,0:T(8,128)S(1)} %copy.93, pred[128,128]{1,0:T(8,128)(4,1)S(1)} %fusion.136, f32[8,256,1,128]{3,2,1,0:T(1,128)} %get-tuple-element.526, s32[]{:T(128)} %get-tuple-element.514), kind=kOutput, calls=%fused_computation.2.clone.1 | convolution fusion | flops 62914560 | bytes 541184 | tf_op jit(solution)/shard_map/while/body/eval_jaxpr/cstu,csu->cst/dot_general | solution.py:119
  226.5 28.5 %fusion.137 = f32[256,1,128]{2,1,0:T(1,128)S(1)} fusion(f32[256,128]{1,0:T(8,128)S(1)} %copy.93, pred[128,128]{1,0:T(8,128)(4,1)S(1)} %fusion.136, f32[8,256,1,128]{3,2,1,0:T(1,128)} %get-tuple-element.526, s32[]{:T(128)} %get-tuple-element.514), kind=kOutput, calls=%fused_computation.2.clone.1 | convolution fusion | flops 62914560 | bytes 541184 | tf_op jit(solution)/shard_map/while/body/eval_jaxpr/cstu,csu->cst/dot_general | solution.py:119
  257.7 28.5 %fusion.137 = f32[256,1,128]{2,1,0:T(1,128)S(1)} fusion(f32[256,128]{1,0:T(8,128)S(1)} %copy.93, pred[128,128]{1,0:T(8,128)(4,1)S(1)} %fusion.136, f32[8,256,1,128]{3,2,1,0:T(1,128)} %get-tuple-element.526, s32[]{:T(128)} %get-tuple-element.514), kind=kOutput, calls=%fused_computation.2.clone.1 | convolution fusion | flops 62914560 | bytes 541184 | tf_op jit(solution)/shard_map/while/body/eval_jaxpr/cstu,csu->cst/dot_general | solution.py:119
  288.8 28.5 %fusion.137 = f32[256,1,128]{2,1,0:T(1,128)S(1)} fusion(f32[256,128]{1,0:T(8,128)S(1)} %copy.93, pred[128,128]{1,0:T(8,128)(4,1)S(1)} %fusion.136, f32[8,256,1,128]{3,2,1,0:T(1,128)} %get-tuple-element.526, s32[]{:T(128)} %get-tuple-element.514), kind=kOutput, calls=%fused_computation.2.clone.1 | convolution fusion | flops 62914560 | bytes 541184 | tf_op jit(solution)/shard_map/while/body/eval_jaxpr/cstu,csu->cst/dot_general | solution.py:119
  320.0 28.5 %fusion.137 = f32[256,1,128]{2,1,0:T(1,128)S(1)} fusion(f32[256,128]{1,0:T(8,128)S(1)} %copy.93, pred[128,128]{1,0:T(8,128)(4,1)S(1)} %fusion.136, f32[8,256,1,128]{3,2,1,0:T(1,128)} %get-tuple-element.526, s32[]{:T(128)} %get-tuple-element.514), kind=kOutput, calls=%fused_computation.2.clone.1 | convolution fusion | flops 62914560 | bytes 541184 | tf_op jit(solution)/shard_map/while/body/eval_jaxpr/cstu,csu->cst/dot_general | solution.py:119
  395.4 629.4 %all-gather.12.cloned.1.call-done = bf16[8192,2048]{1,0:T(8,128)(2,1)} async-done(((bf16[1024,2048]{1,0:T(8,128)(2,1)}), bf16[8192,2048]{1,0:T(8,128)(2,1)}) %all-gather.12.cloned.1.call-update) | async-done | bytes 33554448 | tf_op jit(solution)/shard_map/all_gather | solution.py:17
  1059.1 40.6 %all-gather.8.cloned.1.call-done = bf16[1024,2048]{1,0:T(8,128)(2,1)} async-done(((bf16[128,2048]{1,0:T(8,128)(2,1)}), bf16[1024,2048]{1,0:T(8,128)(2,1)}) %all-gather.8.cloned.1.call-update) | async-done | bytes 4194320 | tf_op jit(solution)/shard_map/all_gather | solution.py:160
  1130.3 78.8 %reduce-scatter.9.cloned.1.call-done = bf16[128,2048]{1,0:T(8,128)(2,1)} async-done(((bf16[1024,2048]{1,0:T(8,128)(2,1)}), bf16[128,2048]{1,0:T(8,128)(2,1)}) %reduce-scatter.9.cloned.1.call-update) | async-done | bytes 524304 | tf_op jit(solution)/shard_map/reduce_scatter | solution.py:174
  1229.4 56.8 %all-gather.10.cloned.1.call-done = bf16[1024,2048]{1,0:T(8,128)(2,1)} async-done(((bf16[128,2048]{1,0:T(8,128)(2,1)}), bf16[1024,2048]{1,0:T(8,128)(2,1)}) %all-gather.10.cloned.1.call-update) | async-done | bytes 4194320 | tf_op jit(solution)/shard_map/all_gather | solution.py:184
  1317.4 183.2 %while.33 = (s32[]{:T(128)}, f32[256,1]{0,1:T(1,128)S(1)}, f32[8,256,1,128]{1,3,2,0:T(8,128)}, f32[8,256,1]{1,2,0:T(1,128)S(1)}, f32[8,1]{0,1:T(1,128)S(1)}, /*i...) while((s32[]{:T(128)}, f32[256,1]{0,1:T(1,128)S(1)}, ...), condition=%wide.region_18.19_spmd.clone.clone, body=%wide.region_17.18_spmd.clone.clone.sunk | while | flops 113853312 | bytes 2405939 | solution.py:207
  1319.2 17.7 fusion.148
  1342.1 17.7 fusion.148
  1364.9 17.7 fusion.148
  1433.5 17.7 fusion.148
  1560.1 46.2 %reduce-scatter.11.cloned.1.call-done = bf16[128,2048]{1,0:T(8,128)(2,1)} async-done(((bf16[1024,2048]{1,0:T(8,128)(2,1)}), bf16[128,2048]{1,0:T(8,128)(2,1)}) %reduce-scatter.11.cloned.1.call-update) | async-done | bytes 524304 | tf_op jit(solution)/shard_map/reduce_scatter | solution.py:232
  1607.8 42.5 %all-reduce.1 = (f32[2048]{0:T(1024)}, f32[2048]{0:T(1024)}, f32[2048]{0:T(1024)}) all-reduce(f32[2048]{0:T(1024)S(1)} %get-tuple-element.358, f32[2048]{0:T(1024)S(1)} %get-tuple-element.354, f32[2048]{0:T(1024)S(1)} %mul.516), channel_id=1, replica_groups=mesh['dp'=4,'mp'=8] {'dp','mp'}, use_global_device_ids=true, to_apply=%region_22.23 | all-reduce | flops 6144 | bytes 49152 | tf_op jit(solution)/shard_map/psum | solution.py:264
  1650.2 48.6 %reduce-scatter.7.cloned.1.call-done = bf16[128,2048]{1,0:T(8,128)(2,1)} async-done(((bf16[1024,2048]{1,0:T(8,128)(2,1)}), bf16[128,2048]{1,0:T(8,128)(2,1)}) %reduce-scatter.7.cloned.1.call-update) | async-done | bytes 524304 | tf_op jit(solution)/shard_map/reduce_scatter | solution.py:150
  1702.5 72.7 %reduce-scatter.13.cloned.1.call-done = bf16[512,2176]{0,1:T(8,128)(2,1)} async-done(((bf16[2048,2176]{0,1:T(8,128)(2,1)}), bf16[512,2176]{0,1:T(8,128)(2,1)}) %reduce-scatter.13.cloned.1.call-update) | async-done | bytes 2228240 | tf_op jit(solution)/shard_map/reduce_scatter | solution.py:246
  1784.9 123.1 %all-reduce.4.cloned.1.call-done = f32[24,2048]{1,0:T(8,128)} async-done(((f32[24,2048]{1,0:T(8,128)}), f32[24,2048]{1,0:T(8,128)}) %all-reduce.4.cloned.1.call-update) | async-done | bytes 196624 | tf_op jit(solution)/shard_map/psum | solution.py:264
  (375 shorter events, 383.6 us)
Async XLA Ops:
  7.2 1092.5 %copy-start = (bf16[704,2048]{1,0:T(8,128)(2,1)S(1)}, bf16[704,2048]{1,0:T(8,128)(2,1)}, u32[]{:S(2)}) copy-start(bf16[704,2048]{1,0:T(8,128)(2,1)} %param.35) | copy-start | bytes 8650756
  7.2 76.9 %all-gather.6.cloned.1.call-start = ((), (), s32[]{:S(2)}) async-start(), calls=%async_computation.6 | async-start | bytes 4718592 | tf_op jit(solution)/shard_map/all_gather | solution.py:76
  7.9 1016.9 %all-gather.12.cloned.1.call-start = ((), (), s32[]{:S(2)}) async-start(), calls=%async_computation.16 | async-start | bytes 37748736 | tf_op jit(solution)/shard_map/all_gather | solution.py:17
  11.4 81.7 %copy-start.24 = (f32[256]{0:T(256)}, f32[256]{0:T(256)S(1)}, u32[]{:S(2)}) copy-start(f32[256]{0:T(256)S(1)} %multiply_reduce_fusion.4) | copy-start | bytes 3076
  11.4 81.7 %copy-start.22 = (f32[256]{0:T(256)}, f32[256]{0:T(256)S(1)}, u32[]{:S(2)}) copy-start(f32[256]{0:T(256)S(1)} %broadcast_subtract_fusion.1) | copy-start | bytes 3076
  13.8 73.5 %copy-start.18 = (f32[2048]{0:T(1024)S(1)}, f32[2048]{0:T(1024)}, u32[]{:S(2)}) copy-start(f32[2048]{0:T(1024)} %param.25) | copy-start | bytes 24580
  100.1 280.4 %copy-start.32 = (f32[256]{0:T(256)S(1)}, f32[256]{0:T(256)}, u32[]{:S(2)}) copy-start(f32[256]{0:T(256)} %param.27) | copy-start | bytes 3076
  387.0 712.7 %all-gather.8.cloned.1.call-start = ((), (), s32[]{:S(2)}) async-start(), calls=%async_computation.8 | async-start | bytes 4718592 | tf_op jit(solution)/shard_map/all_gather | solution.py:160
  387.7 821.4 %reduce-scatter.9.cloned.1.call-start = ((), (), s32[]{:S(2)}) async-start(), calls=%async_computation.9 | async-start | bytes 4718592 | tf_op jit(solution)/shard_map/reduce_scatter | solution.py:174
  1039.4 8.2 copy-start.3
  1039.4 8.2 copy-start.5
  1039.4 8.2 copy-start.17
  1121.7 164.4 %all-gather.10.cloned.1.call-start = ((), (), s32[]{:S(2)}) async-start(), calls=%async_computation.10 | async-start | bytes 4718592 | tf_op jit(solution)/shard_map/all_gather | solution.py:184
  1213.7 341.1 %reduce-scatter.17.cloned.1.call-start = ((), (), s32[]{:S(2)}) async-start(), calls=%async_computation.15 | async-start | bytes 3604480 | tf_op jit(solution)/shard_map/reduce_scatter | solution.py:256
  1221.3 337.0 %reduce-scatter.15.cloned.1.call-start = ((), (), s32[]{:S(2)}) async-start(), calls=%async_computation.14 | async-start | bytes 1310720 | tf_op jit(solution)/shard_map/reduce_scatter | solution.py:253
  1316.3 290.0 %reduce-scatter.11.cloned.1.call-start = ((), (), s32[]{:S(2)}) async-start(), calls=%async_computation.11 | async-start | bytes 4718592 | tf_op jit(solution)/shard_map/reduce_scatter | solution.py:232
  1518.1 180.8 %reduce-scatter.7.cloned.1.call-start = ((), (), s32[]{:S(2)}) async-start(), calls=%async_computation.7 | async-start | bytes 4718592 | tf_op jit(solution)/shard_map/reduce_scatter | solution.py:150
  1524.5 13.6 copy-start.19
  1524.5 13.6 copy-start.31
  1524.5 250.6 %reduce-scatter.13.cloned.1.call-start = ((), (), s32[]{:S(2)}) async-start(), calls=%async_computation.13 | async-start | bytes 11141120 | tf_op jit(solution)/shard_map/reduce_scatter | solution.py:246
  1524.6 13.6 copy-start.6
  1524.6 13.6 copy-start.14
  1524.6 13.6 copy-start.16
  1553.6 354.4 %all-reduce.4.cloned.1.call-start = ((), (), s32[]{:S(2)}) async-start(), calls=%async_computation.12 | async-start | bytes 393216 | tf_op jit(solution)/shard_map/psum | solution.py:264
  (24 other events, 77.2 us)
Sparse Core Ops, SparseCore 0:
  10.2 73.8 all-gather.5
  387.1 637.6 all-gather.11
  1026.9 72.7 all-gather.7
  1121.9 87.1 reduce-scatter.8
  1213.8 72.2 all-gather.9
  1288.7 34.3 reduce-scatter.16
  1325.6 24.8 reduce-scatter.14
  1518.2 88.0 reduce-scatter.10
  1609.9 88.8 reduce-scatter.6
  1701.5 73.6 reduce-scatter.12
  1782.2 125.7 all-reduce.3
